TPU v7x, 128 devices: a whole 4x4x4 slice. The times are simulated.
128 devices in a mesh: ma: 32 (over z, x, core), band: 4 (over y).
Axes of the slice: x: 4, y: 4, z: 4, core: 2. Of those that a mesh axis runs over, the one named last changes fastest.
Arguments:
- observed: bfloat16 [1024, 64, 1024], P(('ma', 'band')), may hold values from -6 to 6
- eigenvalues: float32 [1024, 1024], P(('ma', 'band')), may hold values from 0.05 to 20
- kl_basis: bfloat16 [1024, 1024, 512], P(('ma', 'band')), may hold values from -0.1875 to 0.1875
- band_deriv: bfloat16 [40, 512, 512], P('band'), may hold values from -0.15625 to 0.15625, as said below
- counts: int32 [1024], P(('ma', 'band')), may hold values from 128 to 1024, as said below
Outputs:
- mode_power: float32 [1024, 40], P('ma', 'band')
- band_power: float32 [40], P('band')
Inputs may be any that keep to these rules, and one draw needn't show every extreme that they name: counts[m] is the number of leading KL modes of m-mode m that are kept; some m-mode keeps 1024 and some keeps 1024 // 8. Each band_deriv[a] is symmetric.
All inputs are finite; a program needn't handle non-finite values.
Results may differ from a plain program's by a relative error of at most 0.0018.
Values may be sent and summed in bfloat16 or wider, within the bound.
A program may use at most 64 MiB of HBM per device.

v0:
```python
import jax
import jax.numpy as jnp
from jax import lax
from jax.sharding import Mesh
from jax.sharding import PartitionSpec as P

MA_BAND = ("ma_0", "ma_1", "ma_2", "band")
MA = ("ma_0", "ma_1", "ma_2")


def from_everyone(x, axis):
    count = lax.axis_size(axis)
    return lax.all_to_all(jnp.broadcast_to(x[None], (count, *x.shape)), axis, 0, 0, tiled=True)


def laid_out(tiles, dim):
    tiles = jnp.moveaxis(tiles, 0, dim)
    shape = tiles.shape
    return tiles.reshape(*shape[:dim], shape[dim] * shape[dim + 1], *shape[dim + 2 :])


def gather_directly(x, axis, dim):
    tiles = from_everyone(x, axis)
    return laid_out(tiles, dim)


def over_axes(x, axes):
    for axis in axes:
        x = lax.psum(x, axis)
    return x


def weigh(observed, eigenvalues, counts):
    position = lax.broadcasted_iota(jnp.int32, eigenvalues.shape, 1)
    inside = position < counts[:, None]
    weights = jnp.where(inside, 1.0 / (1.0 + eigenvalues), jnp.zeros_like(eigenvalues))
    return (observed.astype(jnp.float32) * weights[:, None, :]).astype(jnp.bfloat16)


def project_padded(weighted, kl_basis):
    return jnp.einsum("msi,miw->msw", weighted, kl_basis, preferred_element_type=jnp.float32)


def band_quadratic(vectors, matrices):
    mode_count = vectors.shape[0]
    flattened = vectors.reshape(mode_count * vectors.shape[1], vectors.shape[2])

    def one_band(matrix):
        mapped = jnp.dot(flattened, matrix, preferred_element_type=jnp.float32)
        return jnp.sum((mapped * flattened).reshape(mode_count, -1), axis=1)

    return lax.map(one_band, matrices)


def per_device(observed, eigenvalues, kl_basis, band_deriv, counts):
    samples = observed.shape[1]
    own_bands = band_deriv.shape[0]
    weighted = weigh(observed, eigenvalues, counts)
    projected = project_padded(weighted, kl_basis)
    projected = projected.astype(jnp.bfloat16)
    quadratic = band_quadratic(gather_directly(projected, "band", 0), band_deriv)
    mode_power = jnp.transpose(quadratic) / samples
    partial_sum = jnp.sum(mode_power, axis=0)
    band_start = lax.axis_index("band") * own_bands
    scattered = jnp.zeros((own_bands * lax.axis_size("band"),), jnp.float32)
    scattered = lax.dynamic_update_slice_in_dim(scattered, partial_sum, band_start, 0)
    every_band, live_total = (
        over_axes(scattered, MA_BAND),
        over_axes(jnp.sum(counts).astype(jnp.float32), MA_BAND),
    )
    band_total = lax.dynamic_slice_in_dim(every_band, band_start, own_bands, 0)
    band_power = observed.shape[2] * band_total / live_total
    return (mode_power, band_power)


def solution(mesh):
    split = Mesh(
        mesh.devices.reshape(4, 4, 2, mesh.shape["band"]), ("ma_0", "ma_1", "ma_2", "band")
    )
    return jax.shard_map(
        per_device,
        mesh=split,
        in_specs=(
            P(MA_BAND, None, None),
            P(MA_BAND, None),
            P(MA_BAND, None, None),
            P("band", None, None),
            P(MA_BAND),
        ),
        out_specs=(P(MA, "band"), P("band")),
        check_vma=False,
    )
```

profile of v0, /device:TPU:0, one launch (start us, length us, event | category | flops | bytes accessed | tf_op | source)
XLA Modules:
  0.0 119.2 jit_solution(1673569421186196398)
XLA Ops:
  0.6 0.8 divide_select_fusion
  1.5 5.2 %convolution_convert_fusion = bf16[8,64,512]{2,1,0:T(8,128)(2,1)S(1)} fusion(bf16[8,1024,512]{2,1,0:T(8,128)(2,1)} %param.9, bf16[8,64,1024]{2,1,0:T(8,128)(2,1)} %param.7, f32[8,1024]{1,0:T(8,128)S(1)} %divide_select_fusion), kind=kOutput, calls=%fused_computation.6 | convolution fusion | flops 538705920 | bytes 9994240 | tf_op jit(solution)/shard_map/msi,miw->msw/dot_general | solution.py:41
  6.7 1.6 %broadcast_in_dim.23 = bf16[4,8,64,512]{3,2,1,0:T(8,128)(2,1)} broadcast(bf16[8,64,512]{2,1,0:T(8,128)(2,1)S(1)} %convolution_convert_fusion), dimensions={1,2,3} | broadcast | bytes 2621440 | tf_op jit(solution)/shard_map/broadcast_in_dim | solution.py:13
  8.3 4.6 %all-to-all-start = ((bf16[4,8,64,512]{3,2,1,0:T(8,128)(2,1)}), bf16[4,8,64,512]{3,2,1,0:T(8,128)(2,1)S(1)}, u32[]{:S(2)}, u32[]{:S(2)}) async-start(bf16[4,8,64,512]{3,2,1,0:T(8,128)(2,1)} %broadcast_in_dim.23), calls=%async_computation | async-start | bytes 4194304 | tf_op jit(solution)/shard_map/all_to_all | solution.py:13
  12.9 0.6 reduce_sum.35
  14.1 25.0 %all-to-all-done = bf16[4,8,64,512]{3,2,1,0:T(8,128)(2,1)S(1)} async-done(((bf16[4,8,64,512]{3,2,1,0:T(8,128)(2,1)}), bf16[4,8,64,512]{3,2,1,0:T(8,128)(2,1)S(1)}, u32[]{:S(2)}, u32[]{:S(2)}) %all-to-all-start) | async-done | bytes 2097184 | tf_op jit(solution)/shard_map/all_to_all | solution.py:13
  39.2 2.5 %copy.9 = bf16[2048,512]{0,1:T(8,128)(2,1)} copy(bf16[2048,512]{1,0:T(8,128)(2,1)S(1)} %bitcast.21) | data formatting | bytes 4194304 | tf_op jit(solution)/shard_map/while | solution.py:52
  41.7 39.3 %while.10 = (s32[]{:T(128)}, f32[10,32]{1,0:T(8,128)S(1)}, bf16[10,512,512]{2,1,0:T(8,128)(2,1)}, bf16[2048,512]{0,1:T(8,128)(2,1)}, s32[]{:T(128)}, /*index=5*/f32[]{:T(128)}, s32[]{:T(128)}) while((s32[]{:T(128)}, f32[10,32]{1,0:T(8,128)S(1)}, bf16[10,512,512]{2,1,0:T(8,128)(2,1)}, bf16[2048,512]{0,1:T(8,128)(2,1)}, s32[]{:T(128)}, ...), condition=%wide.region_3.4_spmd, body=%wide.region_0.3_spmd.sunk | while | flops 1076887552 | bytes 4752341 | solution.py:52
  41.7 3.7 %fusion.12 = f32[2048]{0:T(1024)S(1)} fusion(bf16[2048,512]{0,1:T(8,128)(2,1)} %get-tuple-element.93, bf16[10,512,512]{2,1,0:T(8,128)(2,1)} %get-tuple-element.92, s32[]{:T(128)} %get-tuple-element.83), kind=kOutput, calls=%fused_computation.1.clone.1 | convolution fusion | flops 1076885504 | bytes 4727296 | tf_op jit(solution)/shard_map/while/body/eval_jaxpr/dot_general | solution.py:49
  45.4 0.1 reduce_sum.43
  45.6 3.7 %fusion.12 = f32[2048]{0:T(1024)S(1)} fusion(bf16[2048,512]{0,1:T(8,128)(2,1)} %get-tuple-element.93, bf16[10,512,512]{2,1,0:T(8,128)(2,1)} %get-tuple-element.92, s32[]{:T(128)} %get-tuple-element.83), kind=kOutput, calls=%fused_computation.1.clone.1 | convolution fusion | flops 1076885504 | bytes 4727296 | tf_op jit(solution)/shard_map/while/body/eval_jaxpr/dot_general | solution.py:49
  49.4 0.1 reduce_sum.43
  49.5 3.7 %fusion.12 = f32[2048]{0:T(1024)S(1)} fusion(bf16[2048,512]{0,1:T(8,128)(2,1)} %get-tuple-element.93, bf16[10,512,512]{2,1,0:T(8,128)(2,1)} %get-tuple-element.92, s32[]{:T(128)} %get-tuple-element.83), kind=kOutput, calls=%fused_computation.1.clone.1 | convolution fusion | flops 1076885504 | bytes 4727296 | tf_op jit(solution)/shard_map/while/body/eval_jaxpr/dot_general | solution.py:49
  53.3 0.1 reduce_sum.43
  53.4 3.7 %fusion.12 = f32[2048]{0:T(1024)S(1)} fusion(bf16[2048,512]{0,1:T(8,128)(2,1)} %get-tuple-element.93, bf16[10,512,512]{2,1,0:T(8,128)(2,1)} %get-tuple-element.92, s32[]{:T(128)} %get-tuple-element.83), kind=kOutput, calls=%fused_computation.1.clone.1 | convolution fusion | flops 1076885504 | bytes 4727296 | tf_op jit(solution)/shard_map/while/body/eval_jaxpr/dot_general | solution.py:49
  57.4 3.7 %fusion.12 = f32[2048]{0:T(1024)S(1)} fusion(bf16[2048,512]{0,1:T(8,128)(2,1)} %get-tuple-element.93, bf16[10,512,512]{2,1,0:T(8,128)(2,1)} %get-tuple-element.92, s32[]{:T(128)} %get-tuple-element.83), kind=kOutput, calls=%fused_computation.1.clone.1 | convolution fusion | flops 1076885504 | bytes 4727296 | tf_op jit(solution)/shard_map/while/body/eval_jaxpr/dot_general | solution.py:49
  61.3 3.7 %fusion.12 = f32[2048]{0:T(1024)S(1)} fusion(bf16[2048,512]{0,1:T(8,128)(2,1)} %get-tuple-element.93, bf16[10,512,512]{2,1,0:T(8,128)(2,1)} %get-tuple-element.92, s32[]{:T(128)} %get-tuple-element.83), kind=kOutput, calls=%fused_computation.1.clone.1 | convolution fusion | flops 1076885504 | bytes 4727296 | tf_op jit(solution)/shard_map/while/body/eval_jaxpr/dot_general | solution.py:49
  65.2 3.7 %fusion.12 = f32[2048]{0:T(1024)S(1)} fusion(bf16[2048,512]{0,1:T(8,128)(2,1)} %get-tuple-element.93, bf16[10,512,512]{2,1,0:T(8,128)(2,1)} %get-tuple-element.92, s32[]{:T(128)} %get-tuple-element.83), kind=kOutput, calls=%fused_computation.1.clone.1 | convolution fusion | flops 1076885504 | bytes 4727296 | tf_op jit(solution)/shard_map/while/body/eval_jaxpr/dot_general | solution.py:49
  69.0 0.1 reduce_sum.43
  69.2 3.7 %fusion.12 = f32[2048]{0:T(1024)S(1)} fusion(bf16[2048,512]{0,1:T(8,128)(2,1)} %get-tuple-element.93, bf16[10,512,512]{2,1,0:T(8,128)(2,1)} %get-tuple-element.92, s32[]{:T(128)} %get-tuple-element.83), kind=kOutput, calls=%fused_computation.1.clone.1 | convolution fusion | flops 1076885504 | bytes 4727296 | tf_op jit(solution)/shard_map/while/body/eval_jaxpr/dot_general | solution.py:49
  72.9 0.1 reduce_sum.43
  73.1 3.7 %fusion.12 = f32[2048]{0:T(1024)S(1)} fusion(bf16[2048,512]{0,1:T(8,128)(2,1)} %get-tuple-element.93, bf16[10,512,512]{2,1,0:T(8,128)(2,1)} %get-tuple-element.92, s32[]{:T(128)} %get-tuple-element.83), kind=kOutput, calls=%fused_computation.1.clone.1 | convolution fusion | flops 1076885504 | bytes 4727296 | tf_op jit(solution)/shard_map/while/body/eval_jaxpr/dot_general | solution.py:49
  76.9 0.1 reduce_sum.43
  77.0 3.7 %fusion.12 = f32[2048]{0:T(1024)S(1)} fusion(bf16[2048,512]{0,1:T(8,128)(2,1)} %get-tuple-element.93, bf16[10,512,512]{2,1,0:T(8,128)(2,1)} %get-tuple-element.92, s32[]{:T(128)} %get-tuple-element.83), kind=kOutput, calls=%fused_computation.1.clone.1 | convolution fusion | flops 1076885504 | bytes 4727296 | tf_op jit(solution)/shard_map/while/body/eval_jaxpr/dot_general | solution.py:49
  80.8 0.1 reduce_sum.43
  81.0 0.7 multiply_reduce_fusion
  81.7 0.2 dynamic_update_slice.7
  81.9 12.3 %all-reduce.2 = (f32[40]{0:T(128)S(1)}, f32[]{:T(128)}) all-reduce(f32[40]{0:T(128)S(1)} %dynamic_update_slice.7, f32[]{:T(128)S(6)} %convert_element_type.18), channel_id=1, replica_groups=mesh['ma_0'=4,'ma_1'=4,'ma_2'=2,'band'=4] {'ma_0'}, use_global_device_ids=true, to_apply=%region_5.6 | all-reduce | flops 41 | bytes 328 | tf_op jit(solution)/shard_map/psum | solution.py:29
  94.2 11.1 %all-reduce.1 = (f32[40]{0:T(128)S(1)}, f32[]{:T(128)}) all-reduce(f32[40]{0:T(128)S(1)} %get-tuple-element.45, f32[]{:T(128)} %get-tuple-element.46), channel_id=1, replica_groups=mesh['ma_0'=4,'ma_1'=4,'ma_2'=2,'band'=4] {'ma_1'}, use_global_device_ids=true, to_apply=%region_6.7 | all-reduce | flops 41 | bytes 328 | tf_op jit(solution)/shard_map/psum | solution.py:29
  105.3 3.1 %all-reduce.3 = (f32[40]{0:T(128)S(1)}, f32[]{:T(128)}) all-reduce(f32[40]{0:T(128)S(1)} %get-tuple-element.43, f32[]{:T(128)} %get-tuple-element.44), channel_id=1, replica_groups=mesh['ma_0'=4,'ma_1'=4,'ma_2'=2,'band'=4] {'ma_2'}, use_global_device_ids=true, to_apply=%region_7.8 | all-reduce | flops 41 | bytes 328 | tf_op jit(solution)/shard_map/psum | solution.py:29
  108.3 9.6 %all-reduce = (f32[40]{0:T(128)S(1)}, f32[]{:T(128)}) all-reduce(f32[40]{0:T(128)S(1)} %get-tuple-element.47, f32[]{:T(128)} %get-tuple-element.48), channel_id=1, replica_groups=mesh['ma_0'=4,'ma_1'=4,'ma_2'=2,'band'=4] {'band'}, use_global_device_ids=true, to_apply=%region_8.9 | all-reduce | flops 41 | bytes 328 | tf_op jit(solution)/shard_map/psum | solution.py:29
  117.9 1.3 %multiply_divide_fusion = f32[10]{0:T(128)} fusion(f32[40]{0:T(128)S(1)} %get-tuple-element.41, s32[]{:T(128)S(6)} %select_n.9, f32[]{:T(128)} %get-tuple-element.42), kind=kLoop, calls=%fused_computation.12 | loop fusion | flops 20 | bytes 88 | tf_op jit(solution)/shard_map/div | solution.py:72
  (27 shorter events, 1.4 us)
Async XLA Ops:
  6.7 6.2 %copy-start = (s32[8]{0:T(128)S(1)}, s32[8]{0:T(128)}, u32[]{:S(2)}) copy-start(s32[8]{0:T(128)} %param.11) | copy-start | bytes 100
  8.3 30.9 %all-to-all-start = ((bf16[4,8,64,512]{3,2,1,0:T(8,128)(2,1)}), bf16[4,8,64,512]{3,2,1,0:T(8,128)(2,1)S(1)}, u32[]{:S(2)}, u32[]{:S(2)}) async-start(bf16[4,8,64,512]{3,2,1,0:T(8,128)(2,1)} %broadcast_in_dim.23), calls=%async_computation | async-start | bytes 4194304 | tf_op jit(solution)/shard_map/all_to_all | solution.py:13
where the time goes:
time: 120 us; the launch traced here: 119 us
  matrix products  42.1 us (35%)
  blocking collectives  36 us (30%)
  waiting for transfers between devices  25 us (21%)
  local copies, waits for them, and re-layouts  5.36 us (4%)
  other arithmetic  4.61 us (4%)
  starting transfers between devices  4.57 us (4%)
  between operations  1.31 us (1%)
    dot_general x10, matrix products, one_band(): mapped = jnp.dot(flattened, matrix, preferred_element_type=jnp.float32)  36.9 us
    psum x4, blocking collectives, over_axes(): x = lax.psum(x, axis)  36 us
    all_to_all x1, waiting for transfers between devices, from_everyone(): lax.all_to_all(jnp.broadcast_to(x[None], (count, *x.shape)), axis, 0, 0,...  25 us
    dot_general x1, matrix products, project_padded(): jnp.einsum('msi,miw->msw', weighted, kl_basis, preferred_element_type=jnp...  5.21 us
    all_to_all x1, starting transfers between devices, from_everyone(): lax.all_to_all(jnp.broadcast_to(x[None], (count, *x.shape)), axis, 0, 0,...  4.57 us
    while x1, local copies, waits for them, and re-layouts, band_quadratic(): return lax.map(one_band, matrices)  2.47 us
  transfers between devices with their start and end apart: 1, of which 1 were waited for; matrix products, arithmetic and copies ran while one was open for 1% of the time, Pallas kernels for 0%

commit v1 on v0

--- a/solution.py
+++ b/solution.py
@@ -26,7 +26,8 @@
 
 def over_axes(x, axes):
     for axis in axes:
-        x = lax.psum(x, axis)
+        parts = lax.all_gather(x, axis)
+        x = jnp.sum(parts, axis=0)
     return x
 
 

time: 120 us -> 122 us (1.017)
  waiting for transfers between devices: 25 us -> 6.25 us
  blocking collectives: 36 us -> 44.6 us
  local copies, waits for them, and re-layouts: 5.36 us -> 13.5 us
  other arithmetic: 4.61 us -> 7.19 us
  between operations: 1.31 us -> 3.27 us
    psum x4 -> x0, blocking collectives: 36 us -> none  [over_axes(): x = lax.psum(x, axis)]
    unnamed x0 -> x4, blocking collectives: none -> 33.6 us
    all_to_all x1, waiting for transfers between devices: 25 us -> 6.25 us  [from_everyone(): lax.all_to_all(jnp.broadcast_to(x[None], (count, *x.shape)), axis, 0, 0,...]
    all_gather x0 -> x1, blocking collectives: none -> 11 us  [over_axes(): parts = lax.all_gather(x, axis)]
    unnamed x2 -> x29, local copies, waits for them, and re-layouts: 0.01 us -> 7.92 us
    reduce_sum x0 -> x8, other arithmetic: none -> 2.58 us  [over_axes(): x = jnp.sum(parts, axis=0)]
  transfers between devices with their start and end apart: 1 -> 1, of which waited for: 1 -> 1; matrix products, arithmetic and copies ran while one was open for 1% -> 5% of each run, Pallas kernels for 0% -> 0%
where the time goes in v1:
time: 122 us
  blocking collectives  44.6 us (37%)
  matrix products  42.1 us (35%)
  local copies, waits for them, and re-layouts  13.5 us (11%)
  other arithmetic  7.19 us (6%)
  waiting for transfers between devices  6.25 us (5%)
  starting transfers between devices  4.57 us (4%)
  between operations  3.27 us (3%)
    dot_general x10, matrix products, one_band(): mapped = jnp.dot(flattened, matrix, preferred_element_type=jnp.float32)  36.9 us
    unnamed x4, blocking collectives  33.6 us
    all_gather x1, blocking collectives, over_axes(): parts = lax.all_gather(x, axis)  11 us
    unnamed x29, local copies, waits for them, and re-layouts  7.92 us
    all_to_all x1, waiting for transfers between devices, from_everyone(): lax.all_to_all(jnp.broadcast_to(x[None], (count, *x.shape)), axis, 0, 0,...  6.25 us
    dot_general x1, matrix products, project_padded(): jnp.einsum('msi,miw->msw', weighted, kl_basis, preferred_element_type=jnp...  5.22 us
    all_to_all x1, starting transfers between devices, from_everyone(): lax.all_to_all(jnp.broadcast_to(x[None], (count, *x.shape)), axis, 0, 0,...  4.57 us
    reduce_sum x8, other arithmetic, over_axes(): x = jnp.sum(parts, axis=0)  2.58 us
  transfers between devices with their start and end apart: 1, of which 1 were waited for; matrix products, arithmetic and copies ran while one was open for 5% of the time, Pallas kernels for 0%

profile of v1, /device:TPU:0, one launch (start us, length us, event | category | flops | bytes accessed | tf_op | source)
XLA Modules:
  0.0 121.6 jit_solution(12237323592387387142)
XLA Ops:
  0.6 0.8 divide_select_fusion
  1.5 5.2 %convolution_convert_fusion = bf16[8,64,512]{2,1,0:T(8,128)(2,1)S(1)} fusion(bf16[8,1024,512]{2,1,0:T(8,128)(2,1)} %param.9, bf16[8,64,1024]{2,1,0:T(8,128)(2,1)} %param.7, f32[8,1024]{1,0:T(8,128)S(1)} %divide_select_fusion), kind=kOutput, calls=%fused_computation.6 | convolution fusion | flops 538705920 | bytes 9994240 | tf_op jit(solution)/shard_map/msi,miw->msw/dot_general | solution.py:42
  6.7 1.6 %broadcast_in_dim.23 = bf16[4,8,64,512]{3,2,1,0:T(8,128)(2,1)} broadcast(bf16[8,64,512]{2,1,0:T(8,128)(2,1)S(1)} %convolution_convert_fusion), dimensions={1,2,3} | broadcast | bytes 2621440 | tf_op jit(solution)/shard_map/broadcast_in_dim | solution.py:13
  8.4 4.6 %all-to-all-start = ((bf16[4,8,64,512]{3,2,1,0:T(8,128)(2,1)}), bf16[4,8,64,512]{3,2,1,0:T(8,128)(2,1)S(1)}, u32[]{:S(2)}, u32[]{:S(2)}) async-start(bf16[4,8,64,512]{3,2,1,0:T(8,128)(2,1)} %broadcast_in_dim.23), calls=%async_computation | async-start | bytes 4194304 | tf_op jit(solution)/shard_map/all_to_all | solution.py:13
  12.9 0.6 reduce_sum.111
  14.8 0.8 dynamic-update-slice.3
  15.6 11.7 %all-reduce.3 = f32[4]{0:T(128)S(1)} all-reduce(f32[4]{0:T(128)S(1)} %dynamic-update-slice.3), channel_id=1, replica_groups=mesh['ma_0'=4,'ma_1'=4,'ma_2'=2,'band'=4] {'ma_0'}, use_global_device_ids=true, to_apply=%add.3 | all-reduce | flops 4 | bytes 32
  29.8 0.6 dynamic-slice.2
  31.0 0.6 reduce_sum.112
  31.6 1.4 %dynamic-update-slice.4 = f32[4]{0:T(128)S(1)} dynamic-update-slice(f32[4]{0:T(128)S(1)} %broadcast.21.clone, f32[1]{0:T(128)} %bitcast.11, u32[]{:T(128)} %bitcast.12) | dynamic-update-slice | bytes 12
  33.0 6.3 %all-to-all-done = bf16[4,8,64,512]{3,2,1,0:T(8,128)(2,1)S(1)} async-done(((bf16[4,8,64,512]{3,2,1,0:T(8,128)(2,1)}), bf16[4,8,64,512]{3,2,1,0:T(8,128)(2,1)S(1)}, u32[]{:S(2)}, u32[]{:S(2)}) %all-to-all-start) | async-done | bytes 2097184 | tf_op jit(solution)/shard_map/all_to_all | solution.py:13
  39.3 2.5 %copy.10 = bf16[2048,512]{0,1:T(8,128)(2,1)} copy(bf16[2048,512]{1,0:T(8,128)(2,1)S(1)} %bitcast.33) | data formatting | bytes 4194304 | tf_op jit(solution)/shard_map/while | solution.py:53
  41.7 39.3 %while.10 = (s32[]{:T(128)}, f32[10,32]{1,0:T(8,128)S(1)}, bf16[10,512,512]{2,1,0:T(8,128)(2,1)}, bf16[2048,512]{0,1:T(8,128)(2,1)}, s32[]{:T(128)}, /*index=5*/f32[]{:T(128)}, s32[]{:T(128)}) while((s32[]{:T(128)}, f32[10,32]{1,0:T(8,128)S(1)}, bf16[10,512,512]{2,1,0:T(8,128)(2,1)}, bf16[2048,512]{0,1:T(8,128)(2,1)}, s32[]{:T(128)}, ...), condition=%wide.region_3.4_spmd, body=%wide.region_0.3_spmd.sunk | while | flops 1076887552 | bytes 4752341 | solution.py:53
  41.7 3.7 %fusion.12 = f32[2048]{0:T(1024)S(1)} fusion(bf16[2048,512]{0,1:T(8,128)(2,1)} %get-tuple-element.95, bf16[10,512,512]{2,1,0:T(8,128)(2,1)} %get-tuple-element.94, s32[]{:T(128)} %get-tuple-element.85), kind=kOutput, calls=%fused_computation.1.clone.1 | convolution fusion | flops 1076885504 | bytes 4727296 | tf_op jit(solution)/shard_map/while/body/eval_jaxpr/dot_general | solution.py:50
  45.7 3.7 %fusion.12 = f32[2048]{0:T(1024)S(1)} fusion(bf16[2048,512]{0,1:T(8,128)(2,1)} %get-tuple-element.95, bf16[10,512,512]{2,1,0:T(8,128)(2,1)} %get-tuple-element.94, s32[]{:T(128)} %get-tuple-element.85), kind=kOutput, calls=%fused_computation.1.clone.1 | convolution fusion | flops 1076885504 | bytes 4727296 | tf_op jit(solution)/shard_map/while/body/eval_jaxpr/dot_general | solution.py:50
  49.6 3.7 %fusion.12 = f32[2048]{0:T(1024)S(1)} fusion(bf16[2048,512]{0,1:T(8,128)(2,1)} %get-tuple-element.95, bf16[10,512,512]{2,1,0:T(8,128)(2,1)} %get-tuple-element.94, s32[]{:T(128)} %get-tuple-element.85), kind=kOutput, calls=%fused_computation.1.clone.1 | convolution fusion | flops 1076885504 | bytes 4727296 | tf_op jit(solution)/shard_map/while/body/eval_jaxpr/dot_general | solution.py:50
  53.5 3.7 %fusion.12 = f32[2048]{0:T(1024)S(1)} fusion(bf16[2048,512]{0,1:T(8,128)(2,1)} %get-tuple-element.95, bf16[10,512,512]{2,1,0:T(8,128)(2,1)} %get-tuple-element.94, s32[]{:T(128)} %get-tuple-element.85), kind=kOutput, calls=%fused_computation.1.clone.1 | convolution fusion | flops 1076885504 | bytes 4727296 | tf_op jit(solution)/shard_map/while/body/eval_jaxpr/dot_general | solution.py:50
  57.4 3.7 %fusion.12 = f32[2048]{0:T(1024)S(1)} fusion(bf16[2048,512]{0,1:T(8,128)(2,1)} %get-tuple-element.95, bf16[10,512,512]{2,1,0:T(8,128)(2,1)} %get-tuple-element.94, s32[]{:T(128)} %get-tuple-element.85), kind=kOutput, calls=%fused_computation.1.clone.1 | convolution fusion | flops 1076885504 | bytes 4727296 | tf_op jit(solution)/shard_map/while/body/eval_jaxpr/dot_general | solution.py:50
  61.4 3.7 %fusion.12 = f32[2048]{0:T(1024)S(1)} fusion(bf16[2048,512]{0,1:T(8,128)(2,1)} %get-tuple-element.95, bf16[10,512,512]{2,1,0:T(8,128)(2,1)} %get-tuple-element.94, s32[]{:T(128)} %get-tuple-element.85), kind=kOutput, calls=%fused_computation.1.clone.1 | convolution fusion | flops 1076885504 | bytes 4727296 | tf_op jit(solution)/shard_map/while/body/eval_jaxpr/dot_general | solution.py:50
  65.3 3.7 %fusion.12 = f32[2048]{0:T(1024)S(1)} fusion(bf16[2048,512]{0,1:T(8,128)(2,1)} %get-tuple-element.95, bf16[10,512,512]{2,1,0:T(8,128)(2,1)} %get-tuple-element.94, s32[]{:T(128)} %get-tuple-element.85), kind=kOutput, calls=%fused_computation.1.clone.1 | convolution fusion | flops 1076885504 | bytes 4727296 | tf_op jit(solution)/shard_map/while/body/eval_jaxpr/dot_general | solution.py:50
  69.2 3.7 %fusion.12 = f32[2048]{0:T(1024)S(1)} fusion(bf16[2048,512]{0,1:T(8,128)(2,1)} %get-tuple-element.95, bf16[10,512,512]{2,1,0:T(8,128)(2,1)} %get-tuple-element.94, s32[]{:T(128)} %get-tuple-element.85), kind=kOutput, calls=%fused_computation.1.clone.1 | convolution fusion | flops 1076885504 | bytes 4727296 | tf_op jit(solution)/shard_map/while/body/eval_jaxpr/dot_general | solution.py:50
  73.2 3.7 %fusion.12 = f32[2048]{0:T(1024)S(1)} fusion(bf16[2048,512]{0,1:T(8,128)(2,1)} %get-tuple-element.95, bf16[10,512,512]{2,1,0:T(8,128)(2,1)} %get-tuple-element.94, s32[]{:T(128)} %get-tuple-element.85), kind=kOutput, calls=%fused_computation.1.clone.1 | convolution fusion | flops 1076885504 | bytes 4727296 | tf_op jit(solution)/shard_map/while/body/eval_jaxpr/dot_general | solution.py:50
  77.1 3.7 %fusion.12 = f32[2048]{0:T(1024)S(1)} fusion(bf16[2048,512]{0,1:T(8,128)(2,1)} %get-tuple-element.95, bf16[10,512,512]{2,1,0:T(8,128)(2,1)} %get-tuple-element.94, s32[]{:T(128)} %get-tuple-element.85), kind=kOutput, calls=%fused_computation.1.clone.1 | convolution fusion | flops 1076885504 | bytes 4727296 | tf_op jit(solution)/shard_map/while/body/eval_jaxpr/dot_general | solution.py:50
  81.0 0.7 multiply_reduce_fusion
  81.9 11.0 %all-gather.3 = f32[4,1,40]{2,1,0:T(1,128)S(1)} all-gather(f32[1,1,40]{2,1,0:T(1,128)S(1)} %dynamic_update_slice.9), channel_id=1, replica_groups=mesh['ma_0'=4,'ma_1'=4,'ma_2'=2,'band'=4] {'ma_0'}, dimensions={0}, use_global_device_ids=true | all-gather | bytes 800 | tf_op jit(solution)/shard_map/all_gather | solution.py:29
  93.2 10.5 %all-reduce.8 = (f32[160]{0:T(256)S(1)}, f32[4]{0:T(128)S(1)}) all-reduce(f32[160]{0:T(256)S(1)} %dynamic-update-slice, f32[4]{0:T(128)S(1)} %dynamic-update-slice.4), channel_id=2, replica_groups=mesh['ma_0'=4,'ma_1'=4,'ma_2'=2,'band'=4] {'ma_1'}, use_global_device_ids=true, to_apply=%add | all-reduce | flops 164 | bytes 1312
  104.5 1.4 %dynamic-update-slice.5 = f32[2]{0:T(128)S(1)} dynamic-update-slice(f32[2]{0:T(128)S(1)} %broadcast.20, f32[1]{0:T(128)} %bitcast.13, u32[]{:T(128)} %bitcast.14) | dynamic-update-slice | bytes 12
  105.9 2.4 %all-reduce.9 = (f32[80]{0:T(128)S(1)}, f32[2]{0:T(128)S(1)}) all-reduce(f32[80]{0:T(128)S(1)} %dynamic-update-slice.1, f32[2]{0:T(128)S(1)} %dynamic-update-slice.5), channel_id=3, replica_groups=mesh['ma_0'=4,'ma_1'=4,'ma_2'=2,'band'=4] {'ma_2'}, use_global_device_ids=true, to_apply=%add.1 | all-reduce | flops 82 | bytes 656
  109.0 1.4 %dynamic-update-slice.6 = f32[4]{0:T(128)S(1)} dynamic-update-slice(f32[4]{0:T(128)S(1)} %broadcast.21, f32[1]{0:T(128)} %bitcast.15, u32[]{:T(128)} %bitcast.16) | dynamic-update-slice | bytes 12
  110.6 9.0 %all-reduce.7 = (f32[160]{0:T(256)S(1)}, f32[4]{0:T(128)S(1)}) all-reduce(f32[160]{0:T(256)S(1)} %dynamic-update-slice.2, f32[4]{0:T(128)S(1)} %dynamic-update-slice.6), channel_id=4, replica_groups=mesh['ma_0'=4,'ma_1'=4,'ma_2'=2,'band'=4] {'band'}, use_global_device_ids=true, to_apply=%add.2 | all-reduce | flops 164 | bytes 1312
  119.7 0.7 reduce_sum.115
  120.4 1.3 %multiply_divide_fusion = f32[10]{0:T(128)} fusion(f32[40]{0:T(128)S(1)} %reduce_sum.110, s32[]{:T(128)S(6)} %select_n.9, f32[]{:T(128)} %reduce_sum.115), kind=kLoop, calls=%fused_computation.12 | loop fusion | flops 20 | bytes 88 | tf_op jit(solution)/shard_map/div | solution.py:73
  (65 shorter events, 6.3 us)
Async XLA Ops:
  6.7 6.2 %copy-start = (s32[8]{0:T(128)S(1)}, s32[8]{0:T(128)}, u32[]{:S(2)}) copy-start(s32[8]{0:T(128)} %param.11) | copy-start | bytes 100
  6.7 7.5 %copy-start.4 = (u32[128]{0:T(128)S(1)}, u32[128]{0:T(128)}, u32[]{:S(2)}) copy-start(u32[128]{0:T(128)} %constant.56) | copy-start | bytes 1540
  6.7 20.6 %copy-start.3 = (u32[128]{0:T(128)S(1)}, u32[128]{0:T(128)}, u32[]{:S(2)}) copy-start(u32[128]{0:T(128)} %constant.41) | copy-start | bytes 1540
  6.7 21.2 %copy-start.2 = (u32[128]{0:T(128)S(1)}, u32[128]{0:T(128)}, u32[]{:S(2)}) copy-start(u32[128]{0:T(128)} %constant.46) | copy-start | bytes 1540
  6.7 23.0 %copy-start.1 = (u32[128]{0:T(128)S(1)}, u32[128]{0:T(128)}, u32[]{:S(2)}) copy-start(u32[128]{0:T(128)} %constant.51) | copy-start | bytes 1540
  8.4 30.9 %all-to-all-start = ((bf16[4,8,64,512]{3,2,1,0:T(8,128)(2,1)}), bf16[4,8,64,512]{3,2,1,0:T(8,128)(2,1)S(1)}, u32[]{:S(2)}, u32[]{:S(2)}) async-start(bf16[4,8,64,512]{3,2,1,0:T(8,128)(2,1)} %broadcast_in_dim.23), calls=%async_computation | async-start | bytes 4194304 | tf_op jit(solution)/shard_map/all_to_all | solution.py:13
